TPU v7x, 32 devices: a whole 2x2x4 slice. The times are simulated.
32 devices in a mesh: seq: 8 (over y, x, core), head: 4 (over z).
Axes of the slice: x: 2, y: 2, z: 4, core: 2. Of those that a mesh axis runs over, the one named last changes fastest.
Arguments:
- projected: bfloat16 [4096, 3, 3072], P(('seq', 'head')), may hold values from -70 to 70
- key_lists: int32 [48, 32, 8], P('head', 'seq'), may hold values from 0 to 31, as said below
- list_counts: int32 [48, 32], P('head', 'seq'), may hold values from 1 to 8
Outputs:
- attended: bfloat16 [4096, 3072], P(('seq', 'head'))
Inputs may be any that keep to these rules, and one draw needn't show every extreme that they name: `key_lists`: entries are key block numbers; no list names its own query block, and the entries of one list are distinct. Entry j of the list of query block b in head h lies on seq shard (b // 4 + o + j) mod 8, o depending on h and b. Over the 12 heads of one head group and the query blocks of one seq shard, exactly 48 entries lie on each seq shard, entries past a list's count included, and the entries that lie on one seq shard name at most two distinct key blocks: at most one whose number within its shard is below 2 and at most one whose number is at least that. In every draw some head group, seq shard and owning seq shard have two.
All inputs are finite; a program needn't handle non-finite values.
Results may differ from a plain program's by a relative error of at most 0.005.
Values may be sent and summed in bfloat16 or wider, within the bound.
No kernel may reach another device: no remote copies, remote signals or barrier semaphores. Data moves between devices by JAX's collectives and lax.ppermute only.
A program may use at most 128 MiB of HBM per device.

v0:
```python
import math
import jax
import jax.numpy as jnp
from jax import lax
from jax.sharding import PartitionSpec as P

NEG_FILL = -1e30


def attend_rows(query_part, gathered, live_cols, head_size):
    row_count, seen_blocks, block_len, doubled = gathered.shape
    key_rows = gathered[..., :head_size].reshape(row_count, seen_blocks * block_len, head_size)
    value_rows = gathered[..., head_size:].reshape(row_count, seen_blocks * block_len, head_size)
    attention_scores = jnp.einsum(
        "rqd,rkd->rqk", query_part, key_rows, preferred_element_type=jnp.float32
    ) * (1.0 / math.sqrt(head_size))
    attention_scores = attention_scores.reshape(row_count, block_len, seen_blocks, block_len)
    attention_scores = jnp.where(live_cols[:, None, :, None], attention_scores, NEG_FILL)
    row_top = jnp.max(attention_scores, axis=(2, 3), keepdims=True)
    exp_scores = jnp.exp(attention_scores - row_top)
    attention_weights = (exp_scores / jnp.sum(exp_scores, axis=(2, 3), keepdims=True)).astype(
        jnp.bfloat16
    )
    attention_weights = attention_weights.reshape(row_count, block_len, seen_blocks * block_len)
    return jnp.einsum(
        "rqk,rkd->rqd", attention_weights, value_rows, preferred_element_type=jnp.float32
    )


def on_device(projected, key_lists, list_counts):
    seq_count = lax.axis_size("seq")
    heads_dev, blocks_dev, list_most = key_lists.shape
    regrouped = lax.all_to_all(projected, "head", split_axis=2, concat_axis=0, tiled=True)
    block_len = regrouped.shape[0] // blocks_dev
    group_width = regrouped.shape[2]
    head_size = group_width // heads_dev
    row_count = heads_dev * blocks_dev
    splitted = regrouped.reshape(blocks_dev, block_len, 3, heads_dev, head_size)
    queries = splitted[:, :, 0].transpose(2, 0, 1, 3).reshape(row_count, block_len, head_size)
    kv_pairs = jnp.concatenate([splitted[:, :, 1], splitted[:, :, 2]], axis=-1)
    kv_pairs = kv_pairs.transpose(2, 0, 1, 3).reshape(row_count, block_len, 2 * head_size)
    entries = key_lists.reshape(row_count * list_most)
    owners = entries // blocks_dev
    row_head = jnp.arange(row_count * list_most, dtype=jnp.int32) // (blocks_dev * list_most)
    capacity = row_count * list_most // seq_count
    wanted = row_head * blocks_dev + entries % blocks_dev
    onehot = (owners[:, None] == jnp.arange(seq_count, dtype=jnp.int32)[None, :]).astype(jnp.int32)
    within = jnp.sum(onehot * (jnp.cumsum(onehot, axis=0) - 1), axis=1)
    slot_ids = owners * capacity + within
    request = (
        jnp.zeros((seq_count * capacity,), jnp.int32)
        .at[slot_ids]
        .set(wanted)
        .reshape(seq_count, capacity)
    )
    asked_for = lax.all_to_all(request, "seq", split_axis=0, concat_axis=0, tiled=True)
    served = jnp.take(kv_pairs, asked_for.reshape(-1), axis=0).reshape(
        seq_count, capacity, block_len, 2 * head_size
    )
    fetched = lax.all_to_all(served, "seq", split_axis=0, concat_axis=0, tiled=True)
    fetched = fetched.reshape(seq_count * capacity, block_len, 2 * head_size)
    entry_slots = slot_ids.reshape(row_count, list_most)
    row_counts = list_counts.reshape(row_count)
    group_rows = 4

    def one_group(group_index):
        start = group_index * group_rows
        query_part = lax.dynamic_slice_in_dim(queries, start, group_rows, 0)
        own_pairs = lax.dynamic_slice_in_dim(kv_pairs, start, group_rows, 0)
        slot_part = lax.dynamic_slice_in_dim(entry_slots, start, group_rows, 0)
        count_part = lax.dynamic_slice_in_dim(row_counts, start, group_rows, 0)
        listed = jnp.take(fetched, slot_part.reshape(-1), axis=0).reshape(
            group_rows, list_most, block_len, 2 * head_size
        )
        gathered = jnp.concatenate([own_pairs[:, None], listed], axis=1)
        live_cols = jnp.concatenate(
            [
                jnp.ones((group_rows, 1), bool),
                jnp.arange(list_most, dtype=jnp.int32)[None, :] < count_part[:, None],
            ],
            axis=1,
        )
        return attend_rows(query_part, gathered, live_cols, head_size).astype(jnp.bfloat16)

    attended = lax.map(one_group, jnp.arange(row_count // group_rows, dtype=jnp.int32))
    attended = attended.reshape(row_count, block_len, head_size)
    laid_out = attended.reshape(heads_dev, blocks_dev * block_len, head_size).transpose(1, 0, 2)
    laid_out = laid_out.reshape(blocks_dev * block_len, group_width)
    return lax.all_to_all(laid_out, "head", split_axis=0, concat_axis=1, tiled=True)


def solution(mesh):
    return jax.shard_map(
        on_device,
        mesh=mesh,
        in_specs=(P(("seq", "head"), None, None), P("head", "seq", None), P("head", "seq")),
        out_specs=P(("seq", "head"), None),
        check_vma=False,
    )
```

profile of v0, /device:TPU:2, one launch (start us, length us, event | category | flops | bytes accessed | tf_op | source)
XLA Modules:
  0.0 542.2 jit_solution(7548757384802746488)
XLA Ops:
  2.4 2.9 scatter_custom_fusion
  6.0 4.3 all-to-all-start.1
  10.3 5.7 %copy.35 = bf16[128,3,3072]{0,1,2:T(4,128)(2,1)} copy(bf16[128,3,3072]{2,0,1:T(8,128)(2,1)} %param.5) | data formatting | bytes 4718592 | tf_op args[0]
  16.0 4.9 all-to-all-start
  22.1 69.7 %all-to-all-done = bf16[128,3,3072]{0,1,2:T(4,128)(2,1)S(1)} async-done(((bf16[128,3,3072]{0,1,2:T(4,128)(2,1)}), bf16[128,3,3072]{0,1,2:T(4,128)(2,1)S(1)}, u32[]{:S(2)}, u32[]{:S(2)}) %all-to-all-start) | async-done | bytes 2359328 | tf_op jit(solution)/shard_map/all_to_all | solution.py:33
  94.5 11.3 %gather_fusion.1 = bf16[384,128,128]{2,1,0:T(8,128)(2,1)} fusion(bf16[48,128,128]{2,1,0:T(8,128)(2,1)S(1)} %bitcast.78, s32[1024]{0:T(1024)S(1)} %pad_clamp_fusion.1), kind=kCustom, calls=%fused_computation.1 | custom fusion | bytes 25167360 | tf_op jit(solution)/shard_map/jit(_take)/gather | solution.py:57
  105.8 10.8 %broadcast_select_fusion.1 = bf16[8,48,128,128]{3,2,1,0:T(8,128)(2,1)} fusion(bf16[8,48,128,128]{3,2,1,0:T(8,128)(2,1)} %bitcast.81, pred[8,48]{1,0:T(8,128)(4,1)S(1)} %compare_and_fusion.1), kind=kLoop, calls=%fused_computation.39 | loop fusion | flops 6291456 | bytes 25166208 | tf_op jit(solution)/shard_map/jit(_take)/select_n | solution.py:57
  116.6 5.7 %all-to-all-start.2 = ((bf16[8,48,128,128]{3,2,1,0:T(8,128)(2,1)}), bf16[8,48,128,128]{3,2,1,0:T(8,128)(2,1)}, u32[]{:S(2)}, u32[]{:S(2)}) async-start(bf16[8,48,128,128]{3,2,1,0:T(8,128)(2,1)} %broadcast_select_fusion.1), calls=%async_computation.2 | async-start | bytes 25165824 | tf_op jit(solution)/shard_map/all_to_all | solution.py:60
  123.6 136.3 %all-to-all-done.2 = bf16[8,48,128,128]{3,2,1,0:T(8,128)(2,1)} async-done(((bf16[8,48,128,128]{3,2,1,0:T(8,128)(2,1)}), bf16[8,48,128,128]{3,2,1,0:T(8,128)(2,1)}, u32[]{:S(2)}, u32[]{:S(2)}) %all-to-all-start.2) | async-done | bytes 12582944 | tf_op jit(solution)/shard_map/all_to_all | solution.py:60
  259.9 256.2 %while.10 = (s32[]{:T(128)}, bf16[12,4,128,64]{2,1,3,0:T(4,128)(2,1)}, s32[12]{0:T(128)S(1)}, s32[48]{0:T(128)S(1)}, bf16[48,128,64]{1,2,0:T(8,128)(2,1)}, /*ind...) while((s32[]{:T(128)}, ...), condition=%wide.region_7.8_spmd, body=%wide.region_4.7_spmd.sunk | while | flops 234721344 | bytes 13664708 | solution.py:85
  261.2 6.3 %gather_fusion = bf16[32,128,128]{2,1,0:T(8,128)(2,1)} fusion(bf16[384,128,128]{2,1,0:T(8,128)(2,1)} %get-tuple-element.162, s32[1024]{0:T(1024)S(1)} %pad_clamp_fusion.3), kind=kCustom, calls=%fused_computation.clone.1 | custom fusion | bytes 2097280 | tf_op jit(solution)/shard_map/while/body/eval_jaxpr/jit(_take)/gather | solution.py:72
  270.6 3.0 fusion.71
  275.4 1.8 fusion.72
  278.4 2.2 fusion.73
  282.6 6.3 %gather_fusion = bf16[32,128,128]{2,1,0:T(8,128)(2,1)} fusion(bf16[384,128,128]{2,1,0:T(8,128)(2,1)} %get-tuple-element.162, s32[1024]{0:T(1024)S(1)} %pad_clamp_fusion.3), kind=kCustom, calls=%fused_computation.clone.1 | custom fusion | bytes 2097280 | tf_op jit(solution)/shard_map/while/body/eval_jaxpr/jit(_take)/gather | solution.py:72
  292.0 3.0 fusion.71
  299.7 2.2 fusion.73
  303.9 6.3 %gather_fusion = bf16[32,128,128]{2,1,0:T(8,128)(2,1)} fusion(bf16[384,128,128]{2,1,0:T(8,128)(2,1)} %get-tuple-element.162, s32[1024]{0:T(1024)S(1)} %pad_clamp_fusion.3), kind=kCustom, calls=%fused_computation.clone.1 | custom fusion | bytes 2097280 | tf_op jit(solution)/shard_map/while/body/eval_jaxpr/jit(_take)/gather | solution.py:72
  313.3 3.0 fusion.71
  321.1 2.2 fusion.73
  325.3 6.3 %gather_fusion = bf16[32,128,128]{2,1,0:T(8,128)(2,1)} fusion(bf16[384,128,128]{2,1,0:T(8,128)(2,1)} %get-tuple-element.162, s32[1024]{0:T(1024)S(1)} %pad_clamp_fusion.3), kind=kCustom, calls=%fused_computation.clone.1 | custom fusion | bytes 2097280 | tf_op jit(solution)/shard_map/while/body/eval_jaxpr/jit(_take)/gather | solution.py:72
  334.7 3.0 fusion.71
  342.4 2.2 fusion.73
  346.6 6.3 %gather_fusion = bf16[32,128,128]{2,1,0:T(8,128)(2,1)} fusion(bf16[384,128,128]{2,1,0:T(8,128)(2,1)} %get-tuple-element.162, s32[1024]{0:T(1024)S(1)} %pad_clamp_fusion.3), kind=kCustom, calls=%fused_computation.clone.1 | custom fusion | bytes 2097280 | tf_op jit(solution)/shard_map/while/body/eval_jaxpr/jit(_take)/gather | solution.py:72
  356.0 3.0 fusion.71
  363.8 2.2 fusion.73
  368.0 6.3 %gather_fusion = bf16[32,128,128]{2,1,0:T(8,128)(2,1)} fusion(bf16[384,128,128]{2,1,0:T(8,128)(2,1)} %get-tuple-element.162, s32[1024]{0:T(1024)S(1)} %pad_clamp_fusion.3), kind=kCustom, calls=%fused_computation.clone.1 | custom fusion | bytes 2097280 | tf_op jit(solution)/shard_map/while/body/eval_jaxpr/jit(_take)/gather | solution.py:72
  377.4 3.0 fusion.71
  385.1 2.2 fusion.73
  389.3 6.3 %gather_fusion = bf16[32,128,128]{2,1,0:T(8,128)(2,1)} fusion(bf16[384,128,128]{2,1,0:T(8,128)(2,1)} %get-tuple-element.162, s32[1024]{0:T(1024)S(1)} %pad_clamp_fusion.3), kind=kCustom, calls=%fused_computation.clone.1 | custom fusion | bytes 2097280 | tf_op jit(solution)/shard_map/while/body/eval_jaxpr/jit(_take)/gather | solution.py:72
  398.7 3.0 fusion.71
  406.4 2.2 fusion.73
  410.7 6.3 %gather_fusion = bf16[32,128,128]{2,1,0:T(8,128)(2,1)} fusion(bf16[384,128,128]{2,1,0:T(8,128)(2,1)} %get-tuple-element.162, s32[1024]{0:T(1024)S(1)} %pad_clamp_fusion.3), kind=kCustom, calls=%fused_computation.clone.1 | custom fusion | bytes 2097280 | tf_op jit(solution)/shard_map/while/body/eval_jaxpr/jit(_take)/gather | solution.py:72
  420.1 3.0 fusion.71
  427.8 2.2 fusion.73
  432.0 6.3 %gather_fusion = bf16[32,128,128]{2,1,0:T(8,128)(2,1)} fusion(bf16[384,128,128]{2,1,0:T(8,128)(2,1)} %get-tuple-element.162, s32[1024]{0:T(1024)S(1)} %pad_clamp_fusion.3), kind=kCustom, calls=%fused_computation.clone.1 | custom fusion | bytes 2097280 | tf_op jit(solution)/shard_map/while/body/eval_jaxpr/jit(_take)/gather | solution.py:72
  441.4 3.0 fusion.71
  449.1 2.2 fusion.73
  453.4 6.3 %gather_fusion = bf16[32,128,128]{2,1,0:T(8,128)(2,1)} fusion(bf16[384,128,128]{2,1,0:T(8,128)(2,1)} %get-tuple-element.162, s32[1024]{0:T(1024)S(1)} %pad_clamp_fusion.3), kind=kCustom, calls=%fused_computation.clone.1 | custom fusion | bytes 2097280 | tf_op jit(solution)/shard_map/while/body/eval_jaxpr/jit(_take)/gather | solution.py:72
  462.8 3.0 fusion.71
  470.5 2.2 fusion.73
  474.7 6.3 %gather_fusion = bf16[32,128,128]{2,1,0:T(8,128)(2,1)} fusion(bf16[384,128,128]{2,1,0:T(8,128)(2,1)} %get-tuple-element.162, s32[1024]{0:T(1024)S(1)} %pad_clamp_fusion.3), kind=kCustom, calls=%fused_computation.clone.1 | custom fusion | bytes 2097280 | tf_op jit(solution)/shard_map/while/body/eval_jaxpr/jit(_take)/gather | solution.py:72
  484.1 3.0 fusion.71
  491.8 2.2 fusion.73
  496.1 6.3 %gather_fusion = bf16[32,128,128]{2,1,0:T(8,128)(2,1)} fusion(bf16[384,128,128]{2,1,0:T(8,128)(2,1)} %get-tuple-element.162, s32[1024]{0:T(1024)S(1)} %pad_clamp_fusion.3), kind=kCustom, calls=%fused_computation.clone.1 | custom fusion | bytes 2097280 | tf_op jit(solution)/shard_map/while/body/eval_jaxpr/jit(_take)/gather | solution.py:72
  505.5 3.0 fusion.71
  513.2 2.2 fusion.73
  518.0 23.0 %all_to_all.48 = bf16[4,128,768]{1,2,0:T(8,128)(2,1)S(1)} all-to-all(bf16[4,128,768]{1,2,0:T(8,128)(2,1)S(1)} %copy.46), channel_id=1, replica_groups=mesh['seq'=8,'head'=4] {'head'}, dimensions={0} | all-to-all | bytes 1572864 | tf_op jit(solution)/shard_map/all_to_all | solution.py:89
  (256 shorter events, 120.1 us)
Async XLA Ops:
  6.0 9.9 %all-to-all-start.1 = ((s32[8,1,48]{2,1,0:T(1,128)}), s32[8,1,48]{2,1,0:T(1,128)S(1)}, u32[]{:S(2)}, u32[]{:S(2)}) async-start(s32[8,1,48]{2,1,0:T(1,128)} %all_to_all.37), calls=%async_computation.1 | async-start | bytes 8192 | tf_op jit(solution)/shard_map/all_to_all | solution.py:56
  16.0 75.9 %all-to-all-start = ((bf16[128,3,3072]{0,1,2:T(4,128)(2,1)}), bf16[128,3,3072]{0,1,2:T(4,128)(2,1)S(1)}, u32[]{:S(2)}, u32[]{:S(2)}) async-start(bf16[128,3,3072]{0,1,2:T(4,128)(2,1)} %copy.35), calls=%async_computation | async-start | bytes 6291456 | tf_op jit(solution)/shard_map/all_to_all | solution.py:33
  116.6 5.8 %copy-start.1 = (s32[12,4]{0,1:T(4,128)S(1)}, s32[12,4]{0,1:T(4,128)}, u32[]{:S(2)}) copy-start(s32[12,4]{0,1:T(4,128)} %param.7) | copy-start | bytes 580
  116.6 6.0 %copy-start = (bf16[12,4,128,64]{2,3,0,1:T(8,128)(2,1)S(1)}, bf16[12,4,128,64]{2,3,0,1:T(8,128)(2,1)}, u32[]{:S(2)}) copy-start(bf16[12,4,128,64]{2,3,0,1:T(8,128)(2,1)} %get-tuple-element.69) | copy-start | bytes 2359300
  116.6 143.3 %all-to-all-start.2 = ((bf16[8,48,128,128]{3,2,1,0:T(8,128)(2,1)}), bf16[8,48,128,128]{3,2,1,0:T(8,128)(2,1)}, u32[]{:S(2)}, u32[]{:S(2)}) async-start(bf16[8,48,128,128]{3,2,1,0:T(8,128)(2,1)} %broadcast_select_fusion.1), calls=%async_computation.2 | async-start | bytes 25165824 | tf_op jit(solution)/shard_map/all_to_all | solution.py:60
where the time goes:
time: 545 us; the launch traced here: 542 us
  waiting for transfers between devices  206 us (38%)
  local copies, waits for them, and re-layouts  178 us (33%)
  other arithmetic  64.3 us (12%)
  matrix products  47.5 us (9%)
  blocking collectives  23 us (4%)
  starting transfers between devices  14.8 us (3%)
  loops' own time  8.01 us (1%)
    all_to_all x1, waiting for transfers between devices, on_device(): lax.all_to_all(served, 'seq', split_axis=0, concat_axis=0, tiled=True)  136 us
    gather x24, local copies, waits for them, and re-layouts, one_group(): jnp.take(fetched, slot_part.reshape(-1), axis=0)  95.7 us
    all_to_all x1, waiting for transfers between devices, on_device(): lax.all_to_all(projected, 'head', split_axis=2, concat_axis=0, tiled=True)  69.7 us
    concatenate x12, other arithmetic, one_group(): gathered = jnp.concatenate([own_pairs[:, None], listed], axis=1)  35.8 us
    dot_general x12, matrix products, attend_rows(): jnp.einsum('rqk,rkd->rqd', attention_weights, value_rows, preferred_eleme...  26.2 us
    all_to_all x1, blocking collectives, on_device(): lax.all_to_all(laid_out, 'head', split_axis=0, concat_axis=1, tiled=True)  23 us
    sub x12, matrix products, attend_rows(): exp_scores = jnp.exp(attention_scores - row_top)  21.2 us
    reshape x12, local copies, waits for them, and re-layouts, attend_rows(): gathered[..., :head_size]  17.7 us
  transfers between devices with their start and end apart: 3, of which 2 were waited for; matrix products, arithmetic and copies ran while one was open for 2% of the time, Pallas kernels for 0%

commit v1 on v0

--- a/solution.py
+++ b/solution.py
@@ -30,7 +30,12 @@
 def on_device(projected, key_lists, list_counts):
     seq_count = lax.axis_size("seq")
     heads_dev, blocks_dev, list_most = key_lists.shape
-    regrouped = lax.all_to_all(projected, "head", split_axis=2, concat_axis=0, tiled=True)
+    regrouped = jnp.concatenate(
+        lax.all_to_all(
+            jnp.stack(jnp.split(projected, lax.axis_size("head"), axis=2)), "head", 0, 0
+        ),
+        axis=0,
+    )
     block_len = regrouped.shape[0] // blocks_dev
     group_width = regrouped.shape[2]
     head_size = group_width // heads_dev

time: 545 us -> 529 us (0.971)
  waiting for transfers between devices: 206 us -> 189 us
    all_to_all x1, waiting for transfers between devices: 69.7 us -> 52.9 us  [on_device(): lax.all_to_all(jnp.stack(jnp.split(projected, lax.axis_size('head'), axis...]
  transfers between devices with their start and end apart: 3 -> 3, of which waited for: 2 -> 2; matrix products, arithmetic and copies ran while one was open for 2% -> 1% of each run, Pallas kernels for 0% -> 0%
where the time goes in v1:
time: 529 us; the launch traced here: 526 us
  waiting for transfers between devices  189 us (36%)
  local copies, waits for them, and re-layouts  177 us (33%)
  other arithmetic  66 us (12%)
  matrix products  47.5 us (9%)
  blocking collectives  23 us (4%)
  starting transfers between devices  14.8 us (3%)
  loops' own time  8.01 us (2%)
    all_to_all x1, waiting for transfers between devices, on_device(): lax.all_to_all(served, 'seq', split_axis=0, concat_axis=0, tiled=True)  136 us
    gather x24, local copies, waits for them, and re-layouts, one_group(): jnp.take(fetched, slot_part.reshape(-1), axis=0)  95.7 us
    all_to_all x1, waiting for transfers between devices, on_device(): lax.all_to_all(jnp.stack(jnp.split(projected, lax.axis_size('head'), axis...  52.9 us
    concatenate x12, other arithmetic, one_group(): gathered = jnp.concatenate([own_pairs[:, None], listed], axis=1)  35.8 us
    dot_general x12, matrix products, attend_rows(): jnp.einsum('rqk,rkd->rqd', attention_weights, value_rows, preferred_eleme...  26.2 us
    all_to_all x1, blocking collectives, on_device(): lax.all_to_all(laid_out, 'head', split_axis=0, concat_axis=1, tiled=True)  23 us
    sub x12, matrix products, attend_rows(): exp_scores = jnp.exp(attention_scores - row_top)  21.2 us
    reshape x12, local copies, waits for them, and re-layouts, attend_rows(): gathered[..., :head_size]  17.7 us
  transfers between devices with their start and end apart: 3, of which 2 were waited for; matrix products, arithmetic and copies ran while one was open for 1% of the time, Pallas kernels for 0%

profile of v1, /device:TPU:2, one launch (start us, length us, event | category | flops | bytes accessed | tf_op | source)
XLA Modules:
  0.0 525.9 jit_solution(17226701897337814916)
XLA Ops:
  2.4 2.9 scatter_custom_fusion
  6.0 4.3 all-to-all-start.1
  15.0 4.9 all-to-all-start
  21.1 52.9 %all-to-all-done = bf16[4,128,3,768]{1,3,2,0:T(8,128)(2,1)} async-done(((bf16[4,128,3,768]{1,3,2,0:T(8,128)(2,1)}), bf16[4,128,3,768]{1,3,2,0:T(8,128)(2,1)}, u32[]{:S(2)}, u32[]{:S(2)}) %all-to-all-start) | async-done | bytes 2359328 | tf_op jit(solution)/shard_map/all_to_all | solution.py:34
  74.1 3.0 slice_bitcast_fusion.1
  78.1 11.3 %gather_fusion.1 = bf16[384,128,128]{2,1,0:T(8,128)(2,1)} fusion(bf16[48,128,128]{2,1,0:T(8,128)(2,1)S(1)} %bitcast.78, s32[1024]{0:T(1024)S(1)} %pad_clamp_fusion.1), kind=kCustom, calls=%fused_computation.1 | custom fusion | bytes 25167360 | tf_op jit(solution)/shard_map/jit(_take)/gather | solution.py:62
  89.5 10.8 %broadcast_select_fusion.1 = bf16[8,48,128,128]{3,2,1,0:T(8,128)(2,1)} fusion(bf16[8,48,128,128]{3,2,1,0:T(8,128)(2,1)} %bitcast.81, pred[8,48]{1,0:T(8,128)(4,1)S(1)} %compare_and_fusion.1), kind=kLoop, calls=%fused_computation.39 | loop fusion | flops 6291456 | bytes 25166208 | tf_op jit(solution)/shard_map/jit(_take)/select_n | solution.py:62
  100.2 5.7 %all-to-all-start.2 = ((bf16[8,48,128,128]{3,2,1,0:T(8,128)(2,1)}), bf16[8,48,128,128]{3,2,1,0:T(8,128)(2,1)}, u32[]{:S(2)}, u32[]{:S(2)}) async-start(bf16[8,48,128,128]{3,2,1,0:T(8,128)(2,1)} %broadcast_select_fusion.1), calls=%async_computation.2 | async-start | bytes 25165824 | tf_op jit(solution)/shard_map/all_to_all | solution.py:65
  107.3 136.3 %all-to-all-done.2 = bf16[8,48,128,128]{3,2,1,0:T(8,128)(2,1)} async-done(((bf16[8,48,128,128]{3,2,1,0:T(8,128)(2,1)}), bf16[8,48,128,128]{3,2,1,0:T(8,128)(2,1)}, u32[]{:S(2)}, u32[]{:S(2)}) %all-to-all-start.2) | async-done | bytes 12582944 | tf_op jit(solution)/shard_map/all_to_all | solution.py:65
  243.6 256.2 %while.10 = (s32[]{:T(128)}, bf16[12,4,128,64]{2,1,3,0:T(4,128)(2,1)}, s32[12]{0:T(128)S(1)}, s32[48]{0:T(128)S(1)}, bf16[48,128,64]{1,2,0:T(8,128)(2,1)}, /*ind...) while((s32[]{:T(128)}, ...), condition=%wide.region_7.8_spmd, body=%wide.region_4.7_spmd.sunk | while | flops 234721344 | bytes 13664708 | solution.py:90
  244.9 6.3 %gather_fusion = bf16[32,128,128]{2,1,0:T(8,128)(2,1)} fusion(bf16[384,128,128]{2,1,0:T(8,128)(2,1)} %get-tuple-element.167, s32[1024]{0:T(1024)S(1)} %pad_clamp_fusion.3), kind=kCustom, calls=%fused_computation.clone.1 | custom fusion | bytes 2097280 | tf_op jit(solution)/shard_map/while/body/eval_jaxpr/jit(_take)/gather | solution.py:77
  254.3 3.0 fusion.72
  259.1 1.8 fusion.73
  262.0 2.2 fusion.74
  266.3 6.3 %gather_fusion = bf16[32,128,128]{2,1,0:T(8,128)(2,1)} fusion(bf16[384,128,128]{2,1,0:T(8,128)(2,1)} %get-tuple-element.167, s32[1024]{0:T(1024)S(1)} %pad_clamp_fusion.3), kind=kCustom, calls=%fused_computation.clone.1 | custom fusion | bytes 2097280 | tf_op jit(solution)/shard_map/while/body/eval_jaxpr/jit(_take)/gather | solution.py:77
  275.7 3.0 fusion.72
  283.4 2.2 fusion.74
  287.6 6.3 %gather_fusion = bf16[32,128,128]{2,1,0:T(8,128)(2,1)} fusion(bf16[384,128,128]{2,1,0:T(8,128)(2,1)} %get-tuple-element.167, s32[1024]{0:T(1024)S(1)} %pad_clamp_fusion.3), kind=kCustom, calls=%fused_computation.clone.1 | custom fusion | bytes 2097280 | tf_op jit(solution)/shard_map/while/body/eval_jaxpr/jit(_take)/gather | solution.py:77
  297.0 3.0 fusion.72
  304.7 2.2 fusion.74
  309.0 6.3 %gather_fusion = bf16[32,128,128]{2,1,0:T(8,128)(2,1)} fusion(bf16[384,128,128]{2,1,0:T(8,128)(2,1)} %get-tuple-element.167, s32[1024]{0:T(1024)S(1)} %pad_clamp_fusion.3), kind=kCustom, calls=%fused_computation.clone.1 | custom fusion | bytes 2097280 | tf_op jit(solution)/shard_map/while/body/eval_jaxpr/jit(_take)/gather | solution.py:77
  318.4 3.0 fusion.72
  326.1 2.2 fusion.74
  330.3 6.3 %gather_fusion = bf16[32,128,128]{2,1,0:T(8,128)(2,1)} fusion(bf16[384,128,128]{2,1,0:T(8,128)(2,1)} %get-tuple-element.167, s32[1024]{0:T(1024)S(1)} %pad_clamp_fusion.3), kind=kCustom, calls=%fused_computation.clone.1 | custom fusion | bytes 2097280 | tf_op jit(solution)/shard_map/while/body/eval_jaxpr/jit(_take)/gather | solution.py:77
  339.7 3.0 fusion.72
  347.4 2.2 fusion.74
  351.7 6.3 %gather_fusion = bf16[32,128,128]{2,1,0:T(8,128)(2,1)} fusion(bf16[384,128,128]{2,1,0:T(8,128)(2,1)} %get-tuple-element.167, s32[1024]{0:T(1024)S(1)} %pad_clamp_fusion.3), kind=kCustom, calls=%fused_computation.clone.1 | custom fusion | bytes 2097280 | tf_op jit(solution)/shard_map/while/body/eval_jaxpr/jit(_take)/gather | solution.py:77
  361.0 3.0 fusion.72
  368.8 2.2 fusion.74
  373.0 6.3 %gather_fusion = bf16[32,128,128]{2,1,0:T(8,128)(2,1)} fusion(bf16[384,128,128]{2,1,0:T(8,128)(2,1)} %get-tuple-element.167, s32[1024]{0:T(1024)S(1)} %pad_clamp_fusion.3), kind=kCustom, calls=%fused_computation.clone.1 | custom fusion | bytes 2097280 | tf_op jit(solution)/shard_map/while/body/eval_jaxpr/jit(_take)/gather | solution.py:77
  382.4 3.0 fusion.72
  390.1 2.2 fusion.74
  394.4 6.3 %gather_fusion = bf16[32,128,128]{2,1,0:T(8,128)(2,1)} fusion(bf16[384,128,128]{2,1,0:T(8,128)(2,1)} %get-tuple-element.167, s32[1024]{0:T(1024)S(1)} %pad_clamp_fusion.3), kind=kCustom, calls=%fused_computation.clone.1 | custom fusion | bytes 2097280 | tf_op jit(solution)/shard_map/while/body/eval_jaxpr/jit(_take)/gather | solution.py:77
  403.7 3.0 fusion.72
  411.5 2.2 fusion.74
  415.7 6.3 %gather_fusion = bf16[32,128,128]{2,1,0:T(8,128)(2,1)} fusion(bf16[384,128,128]{2,1,0:T(8,128)(2,1)} %get-tuple-element.167, s32[1024]{0:T(1024)S(1)} %pad_clamp_fusion.3), kind=kCustom, calls=%fused_computation.clone.1 | custom fusion | bytes 2097280 | tf_op jit(solution)/shard_map/while/body/eval_jaxpr/jit(_take)/gather | solution.py:77
  425.1 3.0 fusion.72
  432.8 2.2 fusion.74
  437.1 6.3 %gather_fusion = bf16[32,128,128]{2,1,0:T(8,128)(2,1)} fusion(bf16[384,128,128]{2,1,0:T(8,128)(2,1)} %get-tuple-element.167, s32[1024]{0:T(1024)S(1)} %pad_clamp_fusion.3), kind=kCustom, calls=%fused_computation.clone.1 | custom fusion | bytes 2097280 | tf_op jit(solution)/shard_map/while/body/eval_jaxpr/jit(_take)/gather | solution.py:77
  446.4 3.0 fusion.72
  454.2 2.2 fusion.74
  458.4 6.3 %gather_fusion = bf16[32,128,128]{2,1,0:T(8,128)(2,1)} fusion(bf16[384,128,128]{2,1,0:T(8,128)(2,1)} %get-tuple-element.167, s32[1024]{0:T(1024)S(1)} %pad_clamp_fusion.3), kind=kCustom, calls=%fused_computation.clone.1 | custom fusion | bytes 2097280 | tf_op jit(solution)/shard_map/while/body/eval_jaxpr/jit(_take)/gather | solution.py:77
  467.8 3.0 fusion.72
  475.5 2.2 fusion.74
  479.7 6.3 %gather_fusion = bf16[32,128,128]{2,1,0:T(8,128)(2,1)} fusion(bf16[384,128,128]{2,1,0:T(8,128)(2,1)} %get-tuple-element.167, s32[1024]{0:T(1024)S(1)} %pad_clamp_fusion.3), kind=kCustom, calls=%fused_computation.clone.1 | custom fusion | bytes 2097280 | tf_op jit(solution)/shard_map/while/body/eval_jaxpr/jit(_take)/gather | solution.py:77
  489.1 3.0 fusion.72
  496.9 2.2 fusion.74
  501.7 23.0 %all_to_all.38 = bf16[4,128,768]{1,2,0:T(8,128)(2,1)S(1)} all-to-all(bf16[4,128,768]{1,2,0:T(8,128)(2,1)S(1)} %copy.56), channel_id=1, replica_groups=mesh['seq'=8,'head'=4] {'head'}, dimensions={0} | all-to-all | bytes 1572864 | tf_op jit(solution)/shard_map/all_to_all | solution.py:94
  (258 shorter events, 123.1 us)
Async XLA Ops:
  6.0 8.9 %all-to-all-start.1 = ((s32[8,1,48]{2,1,0:T(1,128)}), s32[8,1,48]{2,1,0:T(1,128)S(1)}, u32[]{:S(2)}, u32[]{:S(2)}) async-start(s32[8,1,48]{2,1,0:T(1,128)} %all_to_all.27), calls=%async_computation.1 | async-start | bytes 8192 | tf_op jit(solution)/shard_map/all_to_all | solution.py:61
  15.0 59.1 %all-to-all-start = ((bf16[4,128,3,768]{1,3,2,0:T(8,128)(2,1)}), bf16[4,128,3,768]{1,3,2,0:T(8,128)(2,1)}, u32[]{:S(2)}, u32[]{:S(2)}) async-start(bf16[4,128,3,768]{1,3,2,0:T(8,128)(2,1)} %pad_maximum_fusion.1), calls=%async_computation | async-start | bytes 4718592 | tf_op jit(solution)/shard_map/all_to_all | solution.py:34
  100.2 5.8 %copy-start.1 = (s32[12,4]{0,1:T(4,128)S(1)}, s32[12,4]{0,1:T(4,128)}, u32[]{:S(2)}) copy-start(s32[12,4]{0,1:T(4,128)} %param.7) | copy-start | bytes 580
  100.2 6.0 %copy-start = (bf16[12,4,128,64]{2,3,0,1:T(8,128)(2,1)S(1)}, bf16[12,4,128,64]{2,3,0,1:T(8,128)(2,1)}, u32[]{:S(2)}) copy-start(bf16[12,4,128,64]{2,3,0,1:T(8,128)(2,1)} %get-tuple-element.70) | copy-start | bytes 2359300
  100.2 143.3 %all-to-all-start.2 = ((bf16[8,48,128,128]{3,2,1,0:T(8,128)(2,1)}), bf16[8,48,128,128]{3,2,1,0:T(8,128)(2,1)}, u32[]{:S(2)}, u32[]{:S(2)}) async-start(bf16[8,48,128,128]{3,2,1,0:T(8,128)(2,1)} %broadcast_select_fusion.1), calls=%async_computation.2 | async-start | bytes 25165824 | tf_op jit(solution)/shard_map/all_to_all | solution.py:65
